TPU v7x, 32 devices: a whole 2x2x4 slice. The times are simulated.
32 devices in a mesh: ctx: 8 (over z, x), ch: 4 (over y, core).
Axes of the slice: x: 2, y: 2, z: 4, core: 2. Of those that a mesh axis runs over, the one named last changes fastest.
Arguments:
- query_input: bfloat16 [4096, 4096], P('ch', 'ctx'), may hold values from -6 to 6
- key_input: bfloat16 [4096, 4096], P('ch', 'ctx'), may hold values from -6 to 6
- value_input: bfloat16 [4096, 4096], P('ch', 'ctx'), may hold values from -6 to 6
- decay_rate: float32 [8, 16], P('ch'), may hold values from 0 to 1, as said below
- residue: float32 [8, 16], P('ch'), may hold values from -1 to 1
- doc_ends: int32 [4], replicated, may hold values from 1 to 4096, as said below
- out_weight: bfloat16 [4096, 4096], P(None, 'ch'), may hold values from -0.09375 to 0.09375
- out_cotangent: bfloat16 [4096, 4096], P('ctx', 'ch'), may hold values from -6 to 6
Outputs:
- query_grad: bfloat16 [4096, 4096], P('ch', 'ctx')
- key_grad: bfloat16 [4096, 4096], P('ch', 'ctx')
- value_grad: bfloat16 [4096, 4096], P('ch', 'ctx')
- weight_grad: float32 [4096, 4096], P('ctx', 'ch')
Inputs may be any that keep to these rules, and one draw needn't show every extreme that they name: `doc_ends`: strictly increasing; the last entry equals 4096. `decay_rate`: positive.
All inputs are finite; a program needn't handle non-finite values.
Results may differ from a plain program's by a relative error of at most 0.0029.
Values may be sent and summed in bfloat16 or wider, within the bound.
A program may use at most 128 MiB of HBM per device.

v0:
```python
import math
import jax
import jax.numpy as jnp
from jax import lax
from jax.sharding import PartitionSpec as P


def passed_along(block, axis, distance):
    devices = range(lax.axis_size(axis))
    route = [(i - distance, i) for i in devices if i - distance in devices]
    return lax.ppermute(block, axis, route)


def local(
    query_input, key_input, value_input, decay_rate, residue, doc_ends, out_weight, out_cotangent
):
    rows_here, length = query_input.shape
    groups = decay_rate.shape[0]
    group_rows = rows_here // groups
    shard_index = lax.axis_index("ctx")
    anchor = shard_index * length
    offsets = jnp.arange(length, dtype=jnp.int32)
    positions = anchor + offsets
    doc_ids = jnp.sum((doc_ends[None, :] <= positions[:, None]).astype(jnp.int32), axis=1)
    previous = jnp.where(shard_index > 0, jnp.sum((doc_ends <= anchor - 1).astype(jnp.int32)), -1)
    row_block = out_weight
    output_grad = lax.psum_scatter(
        lax.dot_general(
            row_block, out_cotangent, (((1,), (1,)), ((), ())), preferred_element_type=jnp.float32
        ),
        "ch",
        scatter_dimension=0,
        tiled=True,
    )
    highest = lax.Precision.HIGHEST
    place = offsets.astype(jnp.float32)
    centre = place - 0.5 * length
    rising = jnp.exp(-centre[None, :, None] * decay_rate[:, None, :]) * residue[:, None, :]
    falling = jnp.exp(centre[None, :, None] * decay_rate[:, None, :])
    kernel = jnp.einsum("gtn,gsn->gts", rising, falling, precision=highest)
    causal = (offsets[:, None] >= offsets[None, :]) & (doc_ids[:, None] == doc_ids[None, :])
    kernel = jnp.where(causal[None, :, :], kernel, 0.0)
    alive_mask = (doc_ids == previous).astype(jnp.float32)
    tail_mask = (doc_ids == doc_ids[-1]).astype(jnp.float32)
    carry_in_map = (
        residue[:, :, None]
        * jnp.exp(-decay_rate[:, :, None] * (place + 1.0)[None, None, :])
        * alive_mask[None, None, :]
    )
    carry_out_map = (
        jnp.exp(-decay_rate[:, :, None] * (length - 1.0 - place)[None, None, :])
        * tail_mask[None, None, :]
    )
    back_out_map = (
        jnp.exp(-decay_rate[:, :, None] * place[None, None, :]) * alive_mask[None, None, :]
    )
    back_in_map = (
        residue[:, :, None]
        * jnp.exp(-decay_rate[:, :, None] * (length - place)[None, None, :])
        * tail_mask[None, None, :]
    )
    transit = jnp.exp(-decay_rate * length) * (doc_ids[-1] == previous).astype(jnp.float32)
    query_f = query_input.astype(jnp.float32)
    key_f = key_input.astype(jnp.float32)
    value_f = value_input.astype(jnp.float32)
    mixed = (key_f * value_f).reshape(groups, group_rows, length)
    signal = (output_grad * query_f).reshape(groups, group_rows, length)
    forward_part = jnp.einsum("gnl,gcl->gnc", carry_out_map, mixed, precision=highest)
    backward_part = jnp.einsum("gnl,gcl->gnc", back_out_map, signal, precision=highest)

    def chain_turn(turn_index, carried):
        ahead, behind = carried
        ahead = passed_along(transit[:, :, None] * ahead + forward_part, "ctx", 1)
        behind = passed_along(transit[:, :, None] * behind + backward_part, "ctx", -1)
        return (ahead, behind)

    start_pair = (jnp.zeros_like(forward_part), jnp.zeros_like(backward_part))
    entering, returning = lax.fori_loop(0, lax.axis_size("ctx") - 1, chain_turn, start_pair)
    filtered = jnp.einsum("gcs,gts->gct", mixed, kernel, precision=highest)
    filtered = filtered + jnp.einsum("gnc,gnt->gct", entering, carry_in_map, precision=highest)
    spread = jnp.einsum("gct,gts->gcs", signal, kernel, precision=highest)
    spread = spread + jnp.einsum("gnc,gns->gcs", returning, back_in_map, precision=highest)
    filtered = filtered.reshape(rows_here, length)
    spread = spread.reshape(rows_here, length)
    gated = (query_f * filtered).astype(jnp.bfloat16)
    query_grad = (output_grad * filtered).astype(jnp.bfloat16)
    key_grad = (spread * value_f).astype(jnp.bfloat16)
    value_grad = (spread * key_f).astype(jnp.bfloat16)
    gathered = lax.all_gather(gated, "ch", axis=0, tiled=True)
    norm_factor = 1.0 / math.sqrt(length * lax.axis_size("ctx"))
    row_block = gathered
    weight_grad = lax.psum_scatter(
        jnp.dot(row_block, out_cotangent, preferred_element_type=jnp.float32) * norm_factor,
        "ctx",
        scatter_dimension=0,
        tiled=True,
    )
    return (query_grad, key_grad, value_grad, weight_grad)


def solution(mesh):
    return jax.shard_map(
        local,
        mesh=mesh,
        in_specs=(
            P("ch", "ctx"),
            P("ch", "ctx"),
            P("ch", "ctx"),
            P("ch", None),
            P("ch", None),
            P(),
            P(None, "ch"),
            P("ctx", "ch"),
        ),
        out_specs=(P("ch", "ctx"), P("ch", "ctx"), P("ch", "ctx"), P("ctx", "ch")),
        check_vma=False,
    )
```

profile of v0, /device:TPU:0, one launch (start us, length us, event | category | flops | bytes accessed | tf_op | source)
XLA Modules:
  0.0 521.5 jit_solution(614125705850805751)
XLA Ops:
  8.4 10.2 %fusion.70 = f32[4096,512]{1,0:T(8,128)} fusion(bf16[4096,1024]{1,0:T(8,128)(2,1)} %param.16, bf16[512,1024]{1,0:T(8,128)(2,1)S(1)} %copy-done), kind=kOutput, calls=%fused_computation.83 | convolution fusion | flops 4294967296 | bytes 17825792 | tf_op jit(solution)/shard_map/dot_general | solution.py:28
  23.4 3.3 fusion.37
  28.3 2.5 fusion.33
  30.8 62.4 %reduce-scatter.3.cloned.1.call-done = f32[1024,512]{1,0:T(8,128)} async-done(((f32[4096,512]{1,0:T(8,128)}), f32[1024,512]{1,0:T(8,128)}) %reduce-scatter.3.cloned.1.call-update) | async-done | bytes 2097168 | tf_op jit(solution)/shard_map/reduce_scatter | solution.py:27
  93.3 2.2 convert_multiply_fusion.1
  95.4 2.5 fusion.29
  97.9 82.0 %while.12 = (s32[]{:T(128)}, f32[2,16,512]{2,1,0:T(8,128)S(1)}, f32[2,16,512]{2,1,0:T(8,128)S(1)}, f32[2,16]{1,0:T(2,128)S(1)}, f32[2,16,512]{2,1,0:T(8,128)}, /*index=5*/f32[2,16,512]{2,1,0:T(8,128)}, s32[]{:T(128)}) while((s32[]{:T(128)}, f32[2,16,512]{2,1,0:T(8,128)S(1)}, f32[2,16,512]{2,1,0:T(8,128)S(1)}, f32[2,16]{1,0:T(2,128)S(1)}, ...), condition=%wide.region_4.5_spmd, body=%wide.region_3.4_spmd.sunk | while | flops 65538 | bytes 917789 | solution.py:78
  98.0 1.6 multiply_add_fusion.3
  99.5 3.3 collective-permute-start
  105.1 4.2 collective-permute-done.1
  109.3 1.6 multiply_add_fusion.3
  110.9 4.3 collective-permute-start
  117.4 4.2 collective-permute-done.1
  123.1 3.4 collective-permute-start
  129.3 3.6 collective-permute-done.1
  134.4 4.3 collective-permute-start
  140.9 4.2 collective-permute-done.1
  146.7 3.4 collective-permute-start
  152.2 4.2 collective-permute-done.1
  158.0 4.4 collective-permute-start
  164.6 4.2 collective-permute-done.1
  170.3 3.3 collective-permute-start
  175.8 4.2 collective-permute-done.1
  180.0 2.7 fusion.24
  182.7 5.4 %fusion.8 = f32[2,512,512]{2,1,0:T(8,128)S(1)} fusion(f32[2,512,512]{2,1,0:T(8,128)S(1)} %fusion.24, f32[2,512,512]{2,1,0:T(8,128)S(1)} %bitcast.24, f32[2,512,512]{2,1,0:T(8,128)} %fusion.37, pred[512,512]{1,0:T(8,128)(4,1)S(1)} %fusion.16), kind=kOutput, calls=%fused_computation.17 | convolution fusion | flops 3222274048 | bytes 8650752 | tf_op jit(solution)/shard_map/gcs,gts->gct/dot_general | solution.py:79
  188.1 2.0 fusion.2
  190.4 31.3 %all-gather.2.cloned.1.call-done = bf16[4096,512]{1,0:T(8,128)(2,1)} async-done(((bf16[1024,512]{1,0:T(8,128)(2,1)}), bf16[4096,512]{1,0:T(8,128)(2,1)}) %all-gather.2.cloned.1.call-update) | async-done | bytes 4194320 | tf_op jit(solution)/shard_map/all_gather | solution.py:89
  221.7 10.3 %broadcast_multiply_fusion = f32[4096,1024]{1,0:T(8,128)} fusion(bf16[4096,512]{1,0:T(8,128)(2,1)} %all-gather.2.cloned.1.call-done, bf16[512,1024]{1,0:T(8,128)(2,1)S(1)} %copy-done), kind=kOutput, calls=%fused_computation.2 | convolution fusion | flops 4299161600 | bytes 22020096 | tf_op jit(solution)/shard_map/dot_general | solution.py:93
  232.7 1.9 fusion.19
  234.6 3.7 fusion.11
  238.3 1.8 fusion
  240.1 274.8 %reduce-scatter.5.cloned.1.call-done = f32[512,1024]{1,0:T(8,128)} async-done(((f32[4096,1024]{1,0:T(8,128)}), f32[512,1024]{1,0:T(8,128)}) %reduce-scatter.5.cloned.1.call-update) | async-done | bytes 2097168 | tf_op jit(solution)/shard_map/reduce_scatter | solution.py:92
  (68 shorter events, 31.0 us)
Async XLA Ops:
  7.2 1.2 copy-start
  7.2 86.1 %reduce-scatter.3.cloned.1.call-start = ((), (), s32[]{:S(2)}) async-start(), calls=%async_computation.2 | async-start | bytes 10485760 | tf_op jit(solution)/shard_map/reduce_scatter | solution.py:27
  18.6 0.7 copy-start.13
  18.6 3.8 copy-start.12
  18.6 4.7 copy-start.10
  18.7 8.0 %copy-start.6 = (bf16[1024,512]{1,0:T(8,128)(2,1)S(1)}, bf16[1024,512]{1,0:T(8,128)(2,1)}, u32[]{:S(2)}) copy-start(bf16[1024,512]{1,0:T(8,128)(2,1)} %param.12) | copy-start | bytes 3145732
  18.7 8.0 %copy-start.8 = (bf16[1024,512]{1,0:T(8,128)(2,1)S(1)}, bf16[1024,512]{1,0:T(8,128)(2,1)}, u32[]{:S(2)}) copy-start(bf16[1024,512]{1,0:T(8,128)(2,1)} %param.11) | copy-start | bytes 3145732
  18.7 203.0 %all-gather.2.cloned.1.call-start = ((), (), s32[]{:S(2)}) async-start(), calls=%async_computation.3 | async-start | bytes 5242880 | tf_op jit(solution)/shard_map/all_gather | solution.py:89
  27.0 1.3 copy-start.1
  99.5 5.6 %collective-permute-start = (f32[2,16,512]{2,1,0:T(8,128)}, f32[2,16,512]{2,1,0:T(8,128)S(1)}, u32[]{:S(2)}, u32[]{:S(2)}) collective-permute-start(f32[2,16,512]{2,1,0:T(8,128)} %get-tuple-element.102), channel_id=1, source_target_pairs={{0,4},{4,8},{8,12},{12,16},{16,20},{20,24},{24,28},{1,5},{5,9},{9,... | collective-permute-start | bytes 196616 | tf_op jit(solution)/shard_map/while/body/eval_jaxpr/ppermute | solution.py:11
  102.9 6.4 %collective-permute-start.1 = (f32[2,16,512]{2,1,0:T(8,128)}, f32[2,16,512]{2,1,0:T(8,128)S(1)}, u32[]{:S(2)}, u32[]{:S(2)}) collective-permute-start(f32[2,16,512]{2,1,0:T(8,128)} %get-tuple-element.103), channel_id=1, source_target_pairs={{4,0},{8,4},{12,8},{16,12},{20,16},{24,20},{28,24},{5,1},{9,5},{13... | collective-permute-start | bytes 196616 | tf_op jit(solution)/shard_map/while/body/eval_jaxpr/ppermute | solution.py:11
  110.9 6.5 %collective-permute-start = (f32[2,16,512]{2,1,0:T(8,128)}, f32[2,16,512]{2,1,0:T(8,128)S(1)}, u32[]{:S(2)}, u32[]{:S(2)}) collective-permute-start(f32[2,16,512]{2,1,0:T(8,128)} %get-tuple-element.102), channel_id=1, source_target_pairs={{0,4},{4,8},{8,12},{12,16},{16,20},{20,24},{24,28},{1,5},{5,9},{9,... | collective-permute-start | bytes 196616 | tf_op jit(solution)/shard_map/while/body/eval_jaxpr/ppermute | solution.py:11
  115.2 6.4 %collective-permute-start.1 = (f32[2,16,512]{2,1,0:T(8,128)}, f32[2,16,512]{2,1,0:T(8,128)S(1)}, u32[]{:S(2)}, u32[]{:S(2)}) collective-permute-start(f32[2,16,512]{2,1,0:T(8,128)} %get-tuple-element.103), channel_id=1, source_target_pairs={{4,0},{8,4},{12,8},{16,12},{20,16},{24,20},{28,24},{5,1},{9,5},{13... | collective-permute-start | bytes 196616 | tf_op jit(solution)/shard_map/while/body/eval_jaxpr/ppermute | solution.py:11
  123.1 6.2 %collective-permute-start = (f32[2,16,512]{2,1,0:T(8,128)}, f32[2,16,512]{2,1,0:T(8,128)S(1)}, u32[]{:S(2)}, u32[]{:S(2)}) collective-permute-start(f32[2,16,512]{2,1,0:T(8,128)} %get-tuple-element.102), channel_id=1, source_target_pairs={{0,4},{4,8},{8,12},{12,16},{16,20},{20,24},{24,28},{1,5},{5,9},{9,... | collective-permute-start | bytes 196616 | tf_op jit(solution)/shard_map/while/body/eval_jaxpr/ppermute | solution.py:11
  126.5 6.4 %collective-permute-start.1 = (f32[2,16,512]{2,1,0:T(8,128)}, f32[2,16,512]{2,1,0:T(8,128)S(1)}, u32[]{:S(2)}, u32[]{:S(2)}) collective-permute-start(f32[2,16,512]{2,1,0:T(8,128)} %get-tuple-element.103), channel_id=1, source_target_pairs={{4,0},{8,4},{12,8},{16,12},{20,16},{24,20},{28,24},{5,1},{9,5},{13... | collective-permute-start | bytes 196616 | tf_op jit(solution)/shard_map/while/body/eval_jaxpr/ppermute | solution.py:11
  134.4 6.5 %collective-permute-start = (f32[2,16,512]{2,1,0:T(8,128)}, f32[2,16,512]{2,1,0:T(8,128)S(1)}, u32[]{:S(2)}, u32[]{:S(2)}) collective-permute-start(f32[2,16,512]{2,1,0:T(8,128)} %get-tuple-element.102), channel_id=1, source_target_pairs={{0,4},{4,8},{8,12},{12,16},{16,20},{20,24},{24,28},{1,5},{5,9},{9,... | collective-permute-start | bytes 196616 | tf_op jit(solution)/shard_map/while/body/eval_jaxpr/ppermute | solution.py:11
  138.7 6.4 %collective-permute-start.1 = (f32[2,16,512]{2,1,0:T(8,128)}, f32[2,16,512]{2,1,0:T(8,128)S(1)}, u32[]{:S(2)}, u32[]{:S(2)}) collective-permute-start(f32[2,16,512]{2,1,0:T(8,128)} %get-tuple-element.103), channel_id=1, source_target_pairs={{4,0},{8,4},{12,8},{16,12},{20,16},{24,20},{28,24},{5,1},{9,5},{13... | collective-permute-start | bytes 196616 | tf_op jit(solution)/shard_map/while/body/eval_jaxpr/ppermute | solution.py:11
  146.7 5.6 %collective-permute-start = (f32[2,16,512]{2,1,0:T(8,128)}, f32[2,16,512]{2,1,0:T(8,128)S(1)}, u32[]{:S(2)}, u32[]{:S(2)}) collective-permute-start(f32[2,16,512]{2,1,0:T(8,128)} %get-tuple-element.102), channel_id=1, source_target_pairs={{0,4},{4,8},{8,12},{12,16},{16,20},{20,24},{24,28},{1,5},{5,9},{9,... | collective-permute-start | bytes 196616 | tf_op jit(solution)/shard_map/while/body/eval_jaxpr/ppermute | solution.py:11
  150.0 6.4 %collective-permute-start.1 = (f32[2,16,512]{2,1,0:T(8,128)}, f32[2,16,512]{2,1,0:T(8,128)S(1)}, u32[]{:S(2)}, u32[]{:S(2)}) collective-permute-start(f32[2,16,512]{2,1,0:T(8,128)} %get-tuple-element.103), channel_id=1, source_target_pairs={{4,0},{8,4},{12,8},{16,12},{20,16},{24,20},{28,24},{5,1},{9,5},{13... | collective-permute-start | bytes 196616 | tf_op jit(solution)/shard_map/while/body/eval_jaxpr/ppermute | solution.py:11
  158.0 6.6 %collective-permute-start = (f32[2,16,512]{2,1,0:T(8,128)}, f32[2,16,512]{2,1,0:T(8,128)S(1)}, u32[]{:S(2)}, u32[]{:S(2)}) collective-permute-start(f32[2,16,512]{2,1,0:T(8,128)} %get-tuple-element.102), channel_id=1, source_target_pairs={{0,4},{4,8},{8,12},{12,16},{16,20},{20,24},{24,28},{1,5},{5,9},{9,... | collective-permute-start | bytes 196616 | tf_op jit(solution)/shard_map/while/body/eval_jaxpr/ppermute | solution.py:11
  162.4 6.4 %collective-permute-start.1 = (f32[2,16,512]{2,1,0:T(8,128)}, f32[2,16,512]{2,1,0:T(8,128)S(1)}, u32[]{:S(2)}, u32[]{:S(2)}) collective-permute-start(f32[2,16,512]{2,1,0:T(8,128)} %get-tuple-element.103), channel_id=1, source_target_pairs={{4,0},{8,4},{12,8},{16,12},{20,16},{24,20},{28,24},{5,1},{9,5},{13... | collective-permute-start | bytes 196616 | tf_op jit(solution)/shard_map/while/body/eval_jaxpr/ppermute | solution.py:11
  170.3 5.5 %collective-permute-start = (f32[2,16,512]{2,1,0:T(8,128)}, f32[2,16,512]{2,1,0:T(8,128)S(1)}, u32[]{:S(2)}, u32[]{:S(2)}) collective-permute-start(f32[2,16,512]{2,1,0:T(8,128)} %get-tuple-element.102), channel_id=1, source_target_pairs={{0,4},{4,8},{8,12},{12,16},{16,20},{20,24},{24,28},{1,5},{5,9},{9,... | collective-permute-start | bytes 196616 | tf_op jit(solution)/shard_map/while/body/eval_jaxpr/ppermute | solution.py:11
  173.6 6.4 %collective-permute-start.1 = (f32[2,16,512]{2,1,0:T(8,128)}, f32[2,16,512]{2,1,0:T(8,128)S(1)}, u32[]{:S(2)}, u32[]{:S(2)}) collective-permute-start(f32[2,16,512]{2,1,0:T(8,128)} %get-tuple-element.103), channel_id=1, source_target_pairs={{4,0},{8,4},{12,8},{16,12},{20,16},{24,20},{28,24},{5,1},{9,5},{13... | collective-permute-start | bytes 196616 | tf_op jit(solution)/shard_map/while/body/eval_jaxpr/ppermute | solution.py:11
  180.0 2.7 copy-start.2
  182.7 5.4 %copy-start.4 = (f32[1024,512]{1,0:T(8,128)S(1)}, f32[1024,512]{1,0:T(8,128)}, u32[]{:S(2)}) copy-start(f32[1024,512]{1,0:T(8,128)} %reduce-scatter.3.cloned.1.call-done) | copy-start | bytes 6291460
  182.7 5.4 %copy-start.5 = (bf16[1024,512]{1,0:T(8,128)(2,1)S(1)}, bf16[1024,512]{1,0:T(8,128)(2,1)}, u32[]{:S(2)}) copy-start(bf16[1024,512]{1,0:T(8,128)(2,1)} %param.10) | copy-start | bytes 3145732
  190.1 324.8 %reduce-scatter.5.cloned.1.call-start = ((), (), s32[]{:S(2)}) async-start(), calls=%async_computation.4 | async-start | bytes 18874368 | tf_op jit(solution)/shard_map/reduce_scatter | solution.py:92
  232.0 0.7 copy-start.11
  232.0 2.5 copy-start.3
  234.5 3.7 copy-start.7
  234.6 3.7 copy-start.9
Sparse Core Ops, SparseCore 0:
  18.8 74.4 reduce-scatter.2
  190.2 31.3 all-gather.1
  232.1 282.7 reduce-scatter.4
where the time goes:
time: 522 us; the launch traced here: 521 us
  waiting for transfers between devices  404 us (77%)
  matrix products  42.5 us (8%)
  starting transfers between devices  35.8 us (7%)
  other arithmetic  19.5 us (4%)
  between operations  15.3 us (3%)
    reduce_scatter x1, waiting for transfers between devices, local(): lax.psum_scatter(jnp.dot(row_block, out_cotangent, preferred_element_type...  275 us
    reduce_scatter x1, waiting for transfers between devices, local(): lax.psum_scatter(lax.dot_general(row_block, out_cotangent, (((1,), (1,)),...  62.4 us
    ppermute x14, waiting for transfers between devices, passed_along(): return lax.ppermute(block, axis, route)  35.5 us
    ppermute x14, starting transfers between devices, passed_along(): return lax.ppermute(block, axis, route)  35.3 us
    all_gather x1, waiting for transfers between devices, local(): gathered = lax.all_gather(gated, 'ch', axis=0, tiled=True)  31.3 us
    add x7, other arithmetic, chain_turn(): transit[:, :, None] * behind + backward_part  11.1 us
  transfers between devices with their start and end apart: 17, of which 17 were waited for; matrix products, arithmetic and copies ran while one was open for 3% of the time, Pallas kernels for 0%

commit v1 on v0

--- a/solution.py
+++ b/solution.py
@@ -86,7 +86,12 @@
     query_grad = (output_grad * filtered).astype(jnp.bfloat16)
     key_grad = (spread * value_f).astype(jnp.bfloat16)
     value_grad = (spread * key_f).astype(jnp.bfloat16)
-    gathered = lax.all_gather(gated, "ch", axis=0, tiled=True)
+    gathered = jnp.concatenate(
+        lax.all_to_all(
+            jnp.stack(lax.psum(1, axis_name="ch") * [gated]), "ch", concat_axis=0, split_axis=0
+        ),
+        axis=0,
+    )
     norm_factor = 1.0 / math.sqrt(length * lax.axis_size("ctx"))
     row_block = gathered
     weight_grad = lax.psum_scatter(

time: 522 us -> 537 us (1.029)
  blocking collectives: 0 us -> 50.7 us
  waiting for transfers between devices: 404 us -> 370 us
    all_to_all x0 -> x1, blocking collectives: none -> 50.7 us  [local(): lax.all_to_all(jnp.stack(lax.psum(1, axis_name='ch') * [gated]), 'ch', co...]
    all_gather x1 -> x0, waiting for transfers between devices: 31.3 us -> none  [local(): gathered = lax.all_gather(gated, 'ch', axis=0, tiled=True)]
  transfers between devices with their start and end apart: 17 -> 16, of which waited for: 17 -> 16; matrix products, arithmetic and copies ran while one was open for 3% -> 3% of each run, Pallas kernels for 0% -> 0%
where the time goes in v1:
time: 537 us; the launch traced here: 536 us
  waiting for transfers between devices  370 us (69%)
  blocking collectives  50.7 us (9%)
  matrix products  40.3 us (8%)
  starting transfers between devices  35.6 us (7%)
  other arithmetic  19.3 us (4%)
  between operations  15.6 us (3%)
    reduce_scatter x1, waiting for transfers between devices, local(): lax.psum_scatter(jnp.dot(row_block, out_cotangent, preferred_element_type...  272 us
    reduce_scatter x1, waiting for transfers between devices, local(): lax.psum_scatter(lax.dot_general(row_block, out_cotangent, (((1,), (1,)),...  62.4 us
    all_to_all x1, blocking collectives, local(): lax.all_to_all(jnp.stack(lax.psum(1, axis_name='ch') * [gated]), 'ch', co...  50.7 us
    ppermute x14, waiting for transfers between devices, passed_along(): return lax.ppermute(block, axis, route)  35.5 us
    ppermute x14, starting transfers between devices, passed_along(): return lax.ppermute(block, axis, route)  35.3 us
    add x7, other arithmetic, chain_turn(): transit[:, :, None] * behind + backward_part  11.2 us
  transfers between devices with their start and end apart: 16, of which 16 were waited for; matrix products, arithmetic and copies ran while one was open for 3% of the time, Pallas kernels for 0%

profile of v1, /device:TPU:0, one launch (start us, length us, event | category | flops | bytes accessed | tf_op | source)
XLA Modules:
  0.0 535.8 jit_solution(3834917065892836863)
XLA Ops:
  8.4 10.2 %fusion.70 = f32[4096,512]{1,0:T(8,128)} fusion(bf16[4096,1024]{1,0:T(8,128)(2,1)} %param.16, bf16[512,1024]{1,0:T(8,128)(2,1)S(1)} %copy-done), kind=kOutput, calls=%fused_computation.83 | convolution fusion | flops 4294967296 | bytes 17825792 | tf_op jit(solution)/shard_map/dot_general | solution.py:28
  23.4 3.3 fusion.37
  28.4 2.5 fusion.33
  30.9 62.4 %reduce-scatter.3.cloned.1.call-done = f32[1024,512]{1,0:T(8,128)} async-done(((f32[4096,512]{1,0:T(8,128)}), f32[1024,512]{1,0:T(8,128)}) %reduce-scatter.3.cloned.1.call-update) | async-done | bytes 2097168 | tf_op jit(solution)/shard_map/reduce_scatter | solution.py:27
  93.3 2.2 convert_multiply_fusion.1
  95.4 2.5 fusion.29
  97.9 82.1 %while.12 = (s32[]{:T(128)}, f32[2,16,512]{2,1,0:T(8,128)S(1)}, f32[2,16,512]{2,1,0:T(8,128)S(1)}, f32[2,16]{1,0:T(2,128)S(1)}, f32[2,16,512]{2,1,0:T(8,128)}, /*index=5*/f32[2,16,512]{2,1,0:T(8,128)}, s32[]{:T(128)}) while((s32[]{:T(128)}, f32[2,16,512]{2,1,0:T(8,128)S(1)}, f32[2,16,512]{2,1,0:T(8,128)S(1)}, f32[2,16]{1,0:T(2,128)S(1)}, ...), condition=%wide.region_4.5_spmd, body=%wide.region_3.4_spmd.sunk | while | flops 65538 | bytes 917789 | solution.py:78
  97.9 1.6 multiply_add_fusion.3
  99.5 3.3 collective-permute-start
  105.1 4.2 collective-permute-done.1
  109.3 1.6 multiply_add_fusion.3
  110.9 4.3 collective-permute-start
  117.4 4.2 collective-permute-done.1
  123.1 3.4 collective-permute-start
  129.3 3.6 collective-permute-done.1
  134.5 4.3 collective-permute-start
  140.9 4.2 collective-permute-done.1
  146.7 3.4 collective-permute-start
  152.3 4.2 collective-permute-done.1
  158.0 4.4 collective-permute-start
  164.6 4.2 collective-permute-done.1
  170.4 3.3 collective-permute-start
  175.9 4.2 collective-permute-done.1
  180.0 2.7 fusion.24
  182.8 5.4 %fusion.8 = f32[2,512,512]{2,1,0:T(8,128)S(1)} fusion(f32[2,512,512]{2,1,0:T(8,128)S(1)} %fusion.24, f32[2,512,512]{2,1,0:T(8,128)S(1)} %bitcast.25, f32[2,512,512]{2,1,0:T(8,128)} %fusion.37, pred[512,512]{1,0:T(8,128)(4,1)S(1)} %fusion.16), kind=kOutput, calls=%fused_computation.17 | convolution fusion | flops 3222274048 | bytes 8650752 | tf_op jit(solution)/shard_map/gcs,gts->gct/dot_general | solution.py:79
  188.2 1.7 fusion.2
  190.3 50.7 %all_to_all.5 = bf16[4,1024,512]{2,1,0:T(8,128)(2,1)S(1)} all-to-all(bf16[4,1024,512]{2,1,0:T(8,128)(2,1)S(1)} %stack.2), channel_id=1, replica_groups=mesh['ctx'=8,'ch'=4] {'ch'}, dimensions={0} | all-to-all | bytes 8388608 | tf_op jit(solution)/shard_map/all_to_all | solution.py:90
  241.0 8.1 %broadcast_multiply_fusion = f32[4096,1024]{1,0:T(8,128)} fusion(bf16[4096,512]{1,0:T(8,128)(2,1)S(1)} %bitcast.26, bf16[512,1024]{1,0:T(8,128)(2,1)S(1)} %copy-done), kind=kOutput, calls=%fused_computation.2 | convolution fusion | flops 4299161600 | bytes 22020096 | tf_op jit(solution)/shard_map/dot_general | solution.py:98
  249.8 1.9 fusion.19
  251.7 3.7 fusion.11
  255.4 1.8 fusion
  257.2 271.7 %reduce-scatter.5.cloned.1.call-done = f32[512,1024]{1,0:T(8,128)} async-done(((f32[4096,1024]{1,0:T(8,128)}), f32[512,1024]{1,0:T(8,128)}) %reduce-scatter.5.cloned.1.call-update) | async-done | bytes 2097168 | tf_op jit(solution)/shard_map/reduce_scatter | solution.py:97
  (67 shorter events, 31.1 us)
Async XLA Ops:
  7.2 1.2 copy-start
  7.2 86.1 %reduce-scatter.3.cloned.1.call-start = ((), (), s32[]{:S(2)}) async-start(), calls=%async_computation.3 | async-start | bytes 10485760 | tf_op jit(solution)/shard_map/reduce_scatter | solution.py:27
  18.6 0.7 copy-start.13
  18.6 3.9 copy-start.12
  18.6 4.8 copy-start.10
  18.7 8.1 %copy-start.6 = (bf16[1024,512]{1,0:T(8,128)(2,1)S(1)}, bf16[1024,512]{1,0:T(8,128)(2,1)}, u32[]{:S(2)}) copy-start(bf16[1024,512]{1,0:T(8,128)(2,1)} %param.12) | copy-start | bytes 3145732
  18.7 8.1 %copy-start.8 = (bf16[1024,512]{1,0:T(8,128)(2,1)S(1)}, bf16[1024,512]{1,0:T(8,128)(2,1)}, u32[]{:S(2)}) copy-start(bf16[1024,512]{1,0:T(8,128)(2,1)} %param.11) | copy-start | bytes 3145732
  18.7 510.2 %reduce-scatter.5.cloned.1.call-start = ((), (), s32[]{:S(2)}) async-start(), calls=%async_computation.4 | async-start | bytes 18874368 | tf_op jit(solution)/shard_map/reduce_scatter | solution.py:97
  27.1 1.3 copy-start.1
  99.5 5.6 %collective-permute-start = (f32[2,16,512]{2,1,0:T(8,128)}, f32[2,16,512]{2,1,0:T(8,128)S(1)}, u32[]{:S(2)}, u32[]{:S(2)}) collective-permute-start(f32[2,16,512]{2,1,0:T(8,128)} %get-tuple-element.102), channel_id=1, source_target_pairs={{0,4},{4,8},{8,12},{12,16},{16,20},{20,24},{24,28},{1,5},{5,9},{9,... | collective-permute-start | bytes 196616 | tf_op jit(solution)/shard_map/while/body/eval_jaxpr/ppermute | solution.py:11
  102.9 6.4 %collective-permute-start.1 = (f32[2,16,512]{2,1,0:T(8,128)}, f32[2,16,512]{2,1,0:T(8,128)S(1)}, u32[]{:S(2)}, u32[]{:S(2)}) collective-permute-start(f32[2,16,512]{2,1,0:T(8,128)} %get-tuple-element.103), channel_id=1, source_target_pairs={{4,0},{8,4},{12,8},{16,12},{20,16},{24,20},{28,24},{5,1},{9,5},{13... | collective-permute-start | bytes 196616 | tf_op jit(solution)/shard_map/while/body/eval_jaxpr/ppermute | solution.py:11
  110.9 6.5 %collective-permute-start = (f32[2,16,512]{2,1,0:T(8,128)}, f32[2,16,512]{2,1,0:T(8,128)S(1)}, u32[]{:S(2)}, u32[]{:S(2)}) collective-permute-start(f32[2,16,512]{2,1,0:T(8,128)} %get-tuple-element.102), channel_id=1, source_target_pairs={{0,4},{4,8},{8,12},{12,16},{16,20},{20,24},{24,28},{1,5},{5,9},{9,... | collective-permute-start | bytes 196616 | tf_op jit(solution)/shard_map/while/body/eval_jaxpr/ppermute | solution.py:11
  115.2 6.4 %collective-permute-start.1 = (f32[2,16,512]{2,1,0:T(8,128)}, f32[2,16,512]{2,1,0:T(8,128)S(1)}, u32[]{:S(2)}, u32[]{:S(2)}) collective-permute-start(f32[2,16,512]{2,1,0:T(8,128)} %get-tuple-element.103), channel_id=1, source_target_pairs={{4,0},{8,4},{12,8},{16,12},{20,16},{24,20},{28,24},{5,1},{9,5},{13... | collective-permute-start | bytes 196616 | tf_op jit(solution)/shard_map/while/body/eval_jaxpr/ppermute | solution.py:11
  123.1 6.2 %collective-permute-start = (f32[2,16,512]{2,1,0:T(8,128)}, f32[2,16,512]{2,1,0:T(8,128)S(1)}, u32[]{:S(2)}, u32[]{:S(2)}) collective-permute-start(f32[2,16,512]{2,1,0:T(8,128)} %get-tuple-element.102), channel_id=1, source_target_pairs={{0,4},{4,8},{8,12},{12,16},{16,20},{20,24},{24,28},{1,5},{5,9},{9,... | collective-permute-start | bytes 196616 | tf_op jit(solution)/shard_map/while/body/eval_jaxpr/ppermute | solution.py:11
  126.5 6.4 %collective-permute-start.1 = (f32[2,16,512]{2,1,0:T(8,128)}, f32[2,16,512]{2,1,0:T(8,128)S(1)}, u32[]{:S(2)}, u32[]{:S(2)}) collective-permute-start(f32[2,16,512]{2,1,0:T(8,128)} %get-tuple-element.103), channel_id=1, source_target_pairs={{4,0},{8,4},{12,8},{16,12},{20,16},{24,20},{28,24},{5,1},{9,5},{13... | collective-permute-start | bytes 196616 | tf_op jit(solution)/shard_map/while/body/eval_jaxpr/ppermute | solution.py:11
  134.5 6.5 %collective-permute-start = (f32[2,16,512]{2,1,0:T(8,128)}, f32[2,16,512]{2,1,0:T(8,128)S(1)}, u32[]{:S(2)}, u32[]{:S(2)}) collective-permute-start(f32[2,16,512]{2,1,0:T(8,128)} %get-tuple-element.102), channel_id=1, source_target_pairs={{0,4},{4,8},{8,12},{12,16},{16,20},{20,24},{24,28},{1,5},{5,9},{9,... | collective-permute-start | bytes 196616 | tf_op jit(solution)/shard_map/while/body/eval_jaxpr/ppermute | solution.py:11
  138.7 6.4 %collective-permute-start.1 = (f32[2,16,512]{2,1,0:T(8,128)}, f32[2,16,512]{2,1,0:T(8,128)S(1)}, u32[]{:S(2)}, u32[]{:S(2)}) collective-permute-start(f32[2,16,512]{2,1,0:T(8,128)} %get-tuple-element.103), channel_id=1, source_target_pairs={{4,0},{8,4},{12,8},{16,12},{20,16},{24,20},{28,24},{5,1},{9,5},{13... | collective-permute-start | bytes 196616 | tf_op jit(solution)/shard_map/while/body/eval_jaxpr/ppermute | solution.py:11
  146.7 5.6 %collective-permute-start = (f32[2,16,512]{2,1,0:T(8,128)}, f32[2,16,512]{2,1,0:T(8,128)S(1)}, u32[]{:S(2)}, u32[]{:S(2)}) collective-permute-start(f32[2,16,512]{2,1,0:T(8,128)} %get-tuple-element.102), channel_id=1, source_target_pairs={{0,4},{4,8},{8,12},{12,16},{16,20},{20,24},{24,28},{1,5},{5,9},{9,... | collective-permute-start | bytes 196616 | tf_op jit(solution)/shard_map/while/body/eval_jaxpr/ppermute | solution.py:11
  150.1 6.4 %collective-permute-start.1 = (f32[2,16,512]{2,1,0:T(8,128)}, f32[2,16,512]{2,1,0:T(8,128)S(1)}, u32[]{:S(2)}, u32[]{:S(2)}) collective-permute-start(f32[2,16,512]{2,1,0:T(8,128)} %get-tuple-element.103), channel_id=1, source_target_pairs={{4,0},{8,4},{12,8},{16,12},{20,16},{24,20},{28,24},{5,1},{9,5},{13... | collective-permute-start | bytes 196616 | tf_op jit(solution)/shard_map/while/body/eval_jaxpr/ppermute | solution.py:11
  158.0 6.6 %collective-permute-start = (f32[2,16,512]{2,1,0:T(8,128)}, f32[2,16,512]{2,1,0:T(8,128)S(1)}, u32[]{:S(2)}, u32[]{:S(2)}) collective-permute-start(f32[2,16,512]{2,1,0:T(8,128)} %get-tuple-element.102), channel_id=1, source_target_pairs={{0,4},{4,8},{8,12},{12,16},{16,20},{20,24},{24,28},{1,5},{5,9},{9,... | collective-permute-start | bytes 196616 | tf_op jit(solution)/shard_map/while/body/eval_jaxpr/ppermute | solution.py:11
  162.4 6.4 %collective-permute-start.1 = (f32[2,16,512]{2,1,0:T(8,128)}, f32[2,16,512]{2,1,0:T(8,128)S(1)}, u32[]{:S(2)}, u32[]{:S(2)}) collective-permute-start(f32[2,16,512]{2,1,0:T(8,128)} %get-tuple-element.103), channel_id=1, source_target_pairs={{4,0},{8,4},{12,8},{16,12},{20,16},{24,20},{28,24},{5,1},{9,5},{13... | collective-permute-start | bytes 196616 | tf_op jit(solution)/shard_map/while/body/eval_jaxpr/ppermute | solution.py:11
  170.4 5.5 %collective-permute-start = (f32[2,16,512]{2,1,0:T(8,128)}, f32[2,16,512]{2,1,0:T(8,128)S(1)}, u32[]{:S(2)}, u32[]{:S(2)}) collective-permute-start(f32[2,16,512]{2,1,0:T(8,128)} %get-tuple-element.102), channel_id=1, source_target_pairs={{0,4},{4,8},{8,12},{12,16},{16,20},{20,24},{24,28},{1,5},{5,9},{9,... | collective-permute-start | bytes 196616 | tf_op jit(solution)/shard_map/while/body/eval_jaxpr/ppermute | solution.py:11
  173.6 6.4 %collective-permute-start.1 = (f32[2,16,512]{2,1,0:T(8,128)}, f32[2,16,512]{2,1,0:T(8,128)S(1)}, u32[]{:S(2)}, u32[]{:S(2)}) collective-permute-start(f32[2,16,512]{2,1,0:T(8,128)} %get-tuple-element.103), channel_id=1, source_target_pairs={{4,0},{8,4},{12,8},{16,12},{20,16},{24,20},{28,24},{5,1},{9,5},{13... | collective-permute-start | bytes 196616 | tf_op jit(solution)/shard_map/while/body/eval_jaxpr/ppermute | solution.py:11
  180.0 2.7 copy-start.2
  182.7 5.5 %copy-start.4 = (f32[1024,512]{1,0:T(8,128)S(1)}, f32[1024,512]{1,0:T(8,128)}, u32[]{:S(2)}) copy-start(f32[1024,512]{1,0:T(8,128)} %reduce-scatter.3.cloned.1.call-done) | copy-start | bytes 6291460
  182.7 5.5 %copy-start.5 = (bf16[1024,512]{1,0:T(8,128)(2,1)S(1)}, bf16[1024,512]{1,0:T(8,128)(2,1)}, u32[]{:S(2)}) copy-start(bf16[1024,512]{1,0:T(8,128)(2,1)} %param.10) | copy-start | bytes 3145732
  249.1 0.7 copy-start.11
  249.1 2.5 copy-start.3
  251.6 3.7 copy-start.7
  251.7 3.7 copy-start.9
Sparse Core Ops, SparseCore 0:
  18.8 74.4 reduce-scatter.2
  249.2 279.6 reduce-scatter.4
